TPU v7x, 32 devices: a whole 2x2x4 slice. The times are simulated.
32 devices in a mesh: sec: 4 (over y, x), gx: 4 (over z), gy: 2 (over core).
Axes of the slice: x: 2, y: 2, z: 4, core: 2. Of those that a mesh axis runs over, the one named last changes fastest.
Arguments:
- driving: float32 [3, 128, 256], P(None, 'gx', 'gy'), may hold values from -6 to 6
- rate_factor: float32 [3, 128, 256], P(None, 'gx', 'gy'), may hold values from 0.5 to 4
- friction_init: float32 [3, 128, 256], P(None, 'gx', 'gy'), may hold values from 0.2 to 2
- ice_mask: int32 [3, 128, 256], P(None, 'gx', 'gy'), may hold values 0 or 1
- grounded_mask: int32 [3, 128, 256], P(None, 'gx', 'gy'), may hold values 0 or 1
- melt: float32 [3, 128, 256], P(None, 'gx', 'gy'), may hold values from 0.1 to 1
- transmissivity: float32 [3, 128, 256], P(None, 'gx', 'gy'), may hold values from 0.5 to 5
- leakage: float32 [3, 128, 256], P(None, 'gx', 'gy'), may hold values from 0.05 to 0.5
- overburden: float32 [3, 128, 256], P(None, 'gx', 'gy'), may hold values from 0.5 to 2
- friction_scale: float32 [3, 128, 256], P(None, 'gx', 'gy'), may hold values from 0.5 to 4
Outputs:
- column_out: float32 [4, 3, 128, 256], P('sec', None, 'gx', 'gy')
All inputs are finite; a program needn't handle non-finite values. No bound on the sum of `ice_mask` or of `grounded_mask` on one device may be relied on, other than what follows from the above.
Results may differ from a plain program's by a relative error of at most 0.00002.
Values sent between devices are 32-bit elements; how exact they have to be, the bound alone decides.
A program may use at most 64 MiB of HBM per device.

v0:
```python
import jax
import jax.numpy as jnp
from jax import lax
from jax.sharding import PartitionSpec as P

LAYERS = 40
PICARD = 2
SWEEPS = 4
VERT = 4.0
FLOOR = 0.25
HEATING = 0.5


def extended(cells, sides, width):
    for axis, dim in sides:
        count = lax.axis_size(axis)
        ends = count - 1
        head = lax.slice_in_dim(cells, 0, width, axis=dim)
        tail = lax.slice_in_dim(cells, cells.shape[dim] - width, cells.shape[dim], axis=dim)
        cells = jnp.concatenate(
            [
                lax.ppermute(tail, axis, [(i, (i + 1) % count) for i in range(ends)]),
                cells,
                lax.ppermute(head, axis, [((i + 1) % count, i) for i in range(ends)]),
            ],
            axis=dim,
        )
    return cells


def ice_core(velocity, x_plus, x_minus, y_plus, y_minus, driving, rate_here, friction, icemask):
    layers = velocity.shape[0]
    vertical = jnp.concatenate([velocity[1:] - velocity[:-1], jnp.zeros_like(velocity[:1])], axis=0)
    strain = (
        vertical * vertical
        + 0.25 * (x_plus - x_minus) ** 2
        + 0.25 * (y_plus - y_minus) ** 2
        + FLOOR
    )
    viscous = rate_here * strain ** (-1.0 / 3.0)
    coupling = VERT * 0.5 * (viscous[:-1] + viscous[1:])
    right_side = driving + viscous * (x_plus + x_minus + y_plus + y_minus)
    ratios = []
    values = []
    for level_k in range(layers):
        pivot_k = 4.0 * viscous[level_k]
        term_k = right_side[level_k]
        if level_k < layers - 1:
            pivot_k = pivot_k + coupling[level_k]
        if level_k > 0:
            pivot_k = pivot_k + coupling[level_k - 1] - coupling[level_k - 1] * ratios[level_k - 1]
            term_k = term_k + coupling[level_k - 1] * values[level_k - 1]
        else:
            pivot_k = pivot_k + friction
        values.append(term_k / pivot_k)
        if level_k < layers - 1:
            ratios.append(coupling[level_k] / pivot_k)
    result = [values[-1]]
    for level_k in range(layers - 2, -1, -1):
        result.insert(0, values[level_k] + ratios[level_k] * result[0])
    return jnp.stack(result) * icemask


def neighbour_views(padded):
    return (padded[:, 2:, 1:-1], padded[:, :-2, 1:-1], padded[:, 1:-1, 2:], padded[:, 1:-1, :-2])


def sweep_padded(press_pad, trans_pad, leakage, source, inside):
    trans_centre = trans_pad[:, 1:-1, 1:-1]
    numerator = source
    denominator = leakage
    for trans_next, press_next in zip(neighbour_views(trans_pad), neighbour_views(press_pad)):
        face_weight = 0.5 * (trans_centre + trans_next)
        numerator = numerator + face_weight * press_next
        denominator = denominator + face_weight
    return jnp.where(inside > 0.5, numerator / (denominator + (1.0 - inside)), 0.0)


def water_solve(pressure, trans_eff, leakage, source):
    depth = SWEEPS
    stacked = jnp.stack([pressure, trans_eff, leakage, source, jnp.ones_like(pressure)])
    fields = extended(stacked, (("gx", 2), ("gy", 3)), depth)
    press_pad = fields[0]
    for sweep_i in range(SWEEPS):
        inner = sweep_i + 1
        trans_pad = fields[1][
            :, sweep_i : fields.shape[2] - sweep_i, sweep_i : fields.shape[3] - sweep_i
        ]
        leak_in = fields[2][:, inner : fields.shape[2] - inner, inner : fields.shape[3] - inner]
        source_in = fields[3][:, inner : fields.shape[2] - inner, inner : fields.shape[3] - inner]
        inside = fields[4][:, inner : fields.shape[2] - inner, inner : fields.shape[3] - inner]
        press_pad = sweep_padded(press_pad, trans_pad, leak_in, source_in, inside)
    return press_pad


def on_device(
    driving,
    rate_factor,
    friction_init,
    ice_mask,
    grounded_mask,
    melt,
    transmissivity,
    leakage,
    overburden,
    friction_scale,
):
    sectors = lax.axis_size("sec") - 1
    section = lax.axis_index("sec")
    is_ice = section < sectors
    strip_index = jnp.minimum(section, sectors - 1)

    def take_strip(values_in):
        return lax.dynamic_index_in_dim(values_in, strip_index, 0, keepdims=False)

    driving_here = take_strip(driving)
    rate_here = take_strip(rate_factor)
    icemask = take_strip(ice_mask).astype(jnp.float32)
    grounded = grounded_mask.astype(jnp.float32)
    friction_all = friction_init * grounded
    friction_here = take_strip(friction_all)
    width_x = driving.shape[1]
    width_y = driving.shape[2]
    velocity = jnp.zeros((LAYERS, width_x, width_y), jnp.float32)
    pressure = overburden
    for picard in range(PICARD):
        padded = extended(velocity, (("gx", 1), ("gy", 2)), 1)
        x_plus, x_minus, y_plus, y_minus = neighbour_views(padded)
        old_velocity = velocity
        fric_now = friction_here
        velocity = lax.cond(
            is_ice,
            lambda: ice_core(
                old_velocity,
                x_plus,
                x_minus,
                y_plus,
                y_minus,
                driving_here,
                rate_here,
                fric_now,
                icemask,
            ),
            lambda: jnp.zeros_like(old_velocity),
        )
        basal_rows = lax.all_gather(velocity[:1], "sec", axis=0, tiled=True)
        sliding = basal_rows[:sectors]
        squared = sliding * sliding
        trans_eff = transmissivity * (1.0 + squared / (1.0 + squared))
        source = melt + HEATING * friction_all * squared
        pressure = water_solve(pressure, trans_eff, leakage, source)
        friction_all = friction_scale * pressure * grounded
        friction_here = take_strip(friction_all)
    ice_stack = jnp.stack([velocity[-1], velocity[0], friction_here])
    column_out = jnp.where(is_ice, ice_stack, pressure)
    return column_out[None]


def solution(mesh):
    in_specs = (
        P(None, "gx", "gy"),
        P(None, "gx", "gy"),
        P(None, "gx", "gy"),
        P(None, "gx", "gy"),
        P(None, "gx", "gy"),
        P(None, "gx", "gy"),
        P(None, "gx", "gy"),
        P(None, "gx", "gy"),
        P(None, "gx", "gy"),
        P(None, "gx", "gy"),
    )
    out_specs = P("sec", None, "gx", "gy")
    return jax.shard_map(
        on_device, mesh=mesh, in_specs=in_specs, out_specs=out_specs, check_vma=False
    )
```

profile of v0, /device:TPU:0, one launch (start us, length us, event | category | flops | bytes accessed | tf_op | source)
XLA Modules:
  0.0 93.6 jit_solution(11888425895050816554)
XLA Ops:
  0.0 1.3 %collective-permute-start = (f32[40,1,128]{2,0,1:T(8,128)S(1)}, f32[40,1,128]{2,0,1:T(8,128)S(1)}, u32[]{:S(2)}, u32[]{:S(2)}) collective-permute-start(f32[40,1,128]{2,0,1:T(8,128)S(1)} %broadcast.6507), channel_id=1, source_target_pairs={{2,0},{4,2},{6,4},{3,1},{5,3},{7,5},{10,8},{12,10},{14,12},{11,9},... | collective-permute-start | bytes 61448 | tf_op jit(solution)/shard_map/ppermute | solution.py:24
  1.3 5.6 %collective-permute-start.1 = (f32[40,1,128]{2,0,1:T(8,128)S(1)}, f32[40,1,128]{2,0,1:T(8,128)S(1)}, u32[]{:S(2)}, u32[]{:S(2)}) collective-permute-start(f32[40,1,128]{2,0,1:T(8,128)S(1)} %broadcast.6507), channel_id=1, source_target_pairs={{0,2},{2,4},{4,6},{1,3},{3,5},{5,7},{8,10},{10,12},{12,14},{9,11},... | collective-permute-start | bytes 61448 | tf_op jit(solution)/shard_map/ppermute | solution.py:22
  6.9 0.8 bitcast_dynamic-update-slice_fusion.5
  7.7 0.8 convert_multiply_fusion
  8.5 0.7 dynamic-slice_bitcast_fusion
  9.4 0.2 fusion.590
  9.6 0.3 copy.56
  9.9 1.3 %collective-permute-start.2 = (f32[40,34,1]{0,2,1:T(1,128)S(1)}, f32[40,34,1]{0,2,1:T(1,128)S(1)}, u32[]{:S(2)}, u32[]{:S(2)}) collective-permute-start(f32[40,34,1]{0,2,1:T(1,128)S(1)} %copy.56), channel_id=1, source_target_pairs={{1,0},{3,2},{5,4},{7,6},{9,8},{11,10},{13,12},{15,14},{17,16},{19,... | collective-permute-start | bytes 16328 | tf_op jit(solution)/shard_map/ppermute | solution.py:24
  11.2 0.3 copy.57
  11.5 3.0 %collective-permute-start.3 = (f32[40,34,1]{0,2,1:T(1,128)S(1)}, f32[40,34,1]{0,2,1:T(1,128)S(1)}, u32[]{:S(2)}, u32[]{:S(2)}) collective-permute-start(f32[40,34,1]{0,2,1:T(1,128)S(1)} %copy.57), channel_id=1, source_target_pairs={{0,1},{2,3},{4,5},{6,7},{8,9},{10,11},{12,13},{14,15},{16,17},{18,... | collective-permute-start | bytes 16328 | tf_op jit(solution)/shard_map/ppermute | solution.py:22
  14.6 0.7 convert_bitcast_fusion
  15.3 0.3 copy.42
  15.6 0.3 copy.44
  15.9 0.4 maximum_maximum_fusion.1
  16.4 3.6 %conditional.2 = (f32[40,32,128]{2,1,0:T(8,128)S(1)}) conditional(s32[]{:T(128)} %convert_element_type.13, () %tuple.32, (f32[32,128]{1,0:T(8,128)S(1)}, f32[32,128]{1,0:T(8,128)S(1)}, f32[40,1,128]{2,0,1:T(8,128)S(1)}, f32[40,1,128]{2,0,1:T(8,128)S(1)}, f32[40,34,129]{2,0,1:T(8,128)S(1)}, /*index=5*/f32[40,34,129]{2,0,1:T(8,128)S(1)}, ...), branch_computations={%region_0.1_spmd, %region_1.2_spmd} | conditional | flops 5099559 | bytes 16611208 | solution.py:131
  16.4 0.5 copy.47
  16.9 0.5 copy.48
  17.4 1.2 %multiply_add_fusion = (f32[40,32,128]{2,1,0:T(8,128)S(1)}, f32[40,32,128]{2,1,0:T(8,128)S(1)}) fusion(f32[40,34,129]{2,1,0:T(8,128)S(1)} %copy.48, f32[40,34,129]{2,1,0:T(8,128)S(1)} %copy.47, f32[40,1,128]{2,1,0:T(1,128)S(1)} %bitcast.49, f32[40,1,128]{2,1,0:T(1,128)S(1)} %bitcast.50, f32[32,128]{1,0:T(8,128)S(1)} %get-tuple-element.145, ...), kind=kLoop, calls=%fused_computation.2 | loop fusion | flops 2457600 | bytes 2695328 | tf_op jit(solution)/shard_map/cond/branch_1_fun/add | solution.py:42
  18.8 0.4 fusion.11
  19.1 0.2 constant_dynamic-update-slice_fusion.39
  20.1 0.6 copy.49
  20.7 1.3 %collective-permute-start.4 = (f32[40,1,128]{0,2,1:T(8,128)S(1)}, f32[40,1,128]{0,2,1:T(8,128)S(1)}, u32[]{:S(2)}, u32[]{:S(2)}) collective-permute-start(f32[40,1,128]{0,2,1:T(8,128)S(1)} %get-tuple-element.434), channel_id=1, source_target_pairs={{2,0},{4,2},{6,4},{3,1},{5,3},{7,5},{10,8},{12,10},{14,12},{11,9},... | collective-permute-start | bytes 61448 | tf_op jit(solution)/shard_map/ppermute | solution.py:24
  22.0 4.6 %collective-permute-start.5 = (f32[40,1,128]{0,2,1:T(8,128)S(1)}, f32[40,1,128]{0,2,1:T(8,128)S(1)}, u32[]{:S(2)}, u32[]{:S(2)}) collective-permute-start(f32[40,1,128]{0,2,1:T(8,128)S(1)} %get-tuple-element.433), channel_id=1, source_target_pairs={{0,2},{2,4},{4,6},{1,3},{3,5},{5,7},{8,10},{10,12},{12,14},{9,11},... | collective-permute-start | bytes 61448 | tf_op jit(solution)/shard_map/ppermute | solution.py:22
  26.6 8.7 %all_gather.6 = f32[4,32,128]{2,1,0:T(8,128)S(1)} all-gather(f32[1,32,128]{2,1,0:T(8,128)S(1)} %slice.2411), channel_id=1, replica_groups=mesh['sec'=4,'gx'=4,'gy'=2] {'sec'}, dimensions={0}, use_global_device_ids=true | all-gather | bytes 81920 | tf_op jit(solution)/shard_map/all_gather | solution.py:146
  35.4 3.5 %collective-permute-start.8 = (f32[5,3,4,128]{3,2,1,0:T(4,128)S(1)}, f32[5,3,4,128]{3,2,1,0:T(4,128)S(1)}, u32[]{:S(2)}, u32[]{:S(2)}) collective-permute-start(f32[5,3,4,128]{3,2,1,0:T(4,128)S(1)} %get-tuple-element.457), channel_id=1, source_target_pairs={{0,2},{2,4},{4,6},{1,3},{3,5},{5,7},{8,10},{10,12},{12,14},{9,11},... | collective-permute-start | bytes 92168 | tf_op jit(solution)/shard_map/ppermute | solution.py:22
  39.0 1.3 %collective-permute-start.9 = (f32[5,3,4,128]{3,2,1,0:T(4,128)S(1)}, f32[5,3,4,128]{3,2,1,0:T(4,128)S(1)}, u32[]{:S(2)}, u32[]{:S(2)}) collective-permute-start(f32[5,3,4,128]{3,2,1,0:T(4,128)S(1)} %get-tuple-element.458), channel_id=1, source_target_pairs={{2,0},{4,2},{6,4},{3,1},{5,3},{7,5},{10,8},{12,10},{14,12},{11,9},... | collective-permute-start | bytes 92168 | tf_op jit(solution)/shard_map/ppermute | solution.py:24
  40.3 0.6 pad_maximum_fusion.9
  40.9 1.3 %collective-permute-start.6 = (f32[40,34,1]{0,2,1:T(1,128)}, f32[40,34,1]{0,2,1:T(1,128)S(1)}, u32[]{:S(2)}, u32[]{:S(2)}) collective-permute-start(f32[40,34,1]{0,2,1:T(1,128)} %get-tuple-element.432), channel_id=1, source_target_pairs={{1,0},{3,2},{5,4},{7,6},{9,8},{11,10},{13,12},{15,14},{17,16},{19,... | collective-permute-start | bytes 16328 | tf_op jit(solution)/shard_map/ppermute | solution.py:24
  42.2 3.6 %collective-permute-start.7 = (f32[40,34,1]{0,2,1:T(1,128)}, f32[40,34,1]{0,2,1:T(1,128)}, u32[]{:S(2)}, u32[]{:S(2)}) collective-permute-start(f32[40,34,1]{0,2,1:T(1,128)} %get-tuple-element.431), channel_id=1, source_target_pairs={{0,1},{2,3},{4,5},{6,7},{8,9},{10,11},{12,13},{14,15},{16,17},{18,... | collective-permute-start | bytes 16328 | tf_op jit(solution)/shard_map/ppermute | solution.py:22
  45.9 0.1 copy.52
  46.0 1.3 %pad_maximum_fusion.3 = (f32[40,33,128]{2,1,0:T(8,128)}, f32[40,33,128]{2,1,0:T(8,128)}) fusion(f32[40,32,128]{2,1,0:T(8,128)S(1)} %get-tuple-element.465, f32[40,1,128]{2,1,0:T(1,128)S(1)} %copy.52, f32[40,1,128]{2,1,0:T(1,128)S(1)} %copy.50), kind=kLoop, calls=%fused_computation.727 | loop fusion | flops 337920 | bytes 2048000 | tf_op jit(solution)/shard_map/concatenate | solution.py:20
  47.4 0.1 fusion.592
  47.5 1.3 %collective-permute-start.10 = (f32[5,3,40,4]{3,2,1,0:T(8,128)S(1)}, f32[5,3,40,4]{3,2,1,0:T(8,128)S(1)}, u32[]{:S(2)}, u32[]{:S(2)}) collective-permute-start(f32[5,3,40,4]{3,2,1,0:T(8,128)S(1)} %get-tuple-element.453), channel_id=1, source_target_pairs={{0,1},{2,3},{4,5},{6,7},{8,9},{10,11},{12,13},{14,15},{16,17},{18,... | collective-permute-start | bytes 28808 | tf_op jit(solution)/shard_map/ppermute | solution.py:22
  48.8 1.3 %collective-permute-start.11 = (f32[5,3,40,4]{3,2,1,0:T(8,128)S(1)}, f32[5,3,40,4]{3,2,1,0:T(8,128)S(1)}, u32[]{:S(2)}, u32[]{:S(2)}) collective-permute-start(f32[5,3,40,4]{3,2,1,0:T(8,128)S(1)} %get-tuple-element.454), channel_id=1, source_target_pairs={{1,0},{3,2},{5,4},{7,6},{9,8},{11,10},{13,12},{15,14},{17,16},{19,... | collective-permute-start | bytes 28808 | tf_op jit(solution)/shard_map/ppermute | solution.py:24
  50.1 3.3 %maximum_maximum_fusion = (f32[40,34,129]{0,2,1:T(8,128)}, f32[40,34,129]{0,2,1:T(8,128)}) fusion(f32[40,1,128]{0,2,1:T(8,128)S(1)} %collective-permute-done.4, f32[40,32,128]{0,2,1:T(8,128)S(1)} %copy.49, f32[40,1,128]{0,2,1:T(8,128)S(1)} %collective-permute-done.5, f32[40,34,1]{0,2,1:T(1,128)} %collective-permute-done.7, ...), kind=kLoop, calls=%fused_computation.723 | loop fusion | flops 1052640 | bytes 2110720 | tf_op jit(solution)/shard_map/concatenate | solution.py:20
  53.4 0.4 pad_maximum_fusion.5
  53.8 0.4 fusion.389
  54.3 0.4 fusion.376
  54.7 0.4 fusion.363
  55.2 0.2 multiply_multiply_fusion
  55.4 0.6 copy-done
  56.0 12.4 %conditional.3 = (f32[1,32,128]{2,1,0:T(8,128)S(1)}, f32[1,32,128]{2,1,0:T(8,128)S(1)}) conditional(s32[]{:T(128)} %convert_element_type.13, () %tuple.31, (f32[32,128]{1,0:T(8,128)S(1)}, f32[32,128]{1,0:T(8,128)S(1)}, f32[40,32,128]{2,1,0:T(8,128)S(1)}, f32[40,33,128]{2,1,0:T(8,128)}, f32[40,33,128]{2,1,0:T(8,128)}, ...), branch_computations={%region_2.3_spmd, %region_3.4_spmd} | conditional | flops 5423103 | bytes 25908556 | solution.py:131
  56.0 4.1 %copy.54 = f32[40,34,129]{2,1,0:T(8,128)} copy(f32[40,34,129]{0,2,1:T(8,128)} %get-tuple-element.220) | data formatting | bytes 1403520 | tf_op jit(solution)/shard_map
  60.1 2.6 %copy.55 = f32[40,34,129]{2,1,0:T(8,128)} copy(f32[40,34,129]{0,2,1:T(8,128)S(1)} %get-tuple-element.221) | data formatting | bytes 1403520 | tf_op jit(solution)/shard_map
  62.7 1.1 %copy-done.1 = f32[40,33,128]{2,1,0:T(8,128)S(1)} copy-done((f32[40,33,128]{2,1,0:T(8,128)S(1)}, f32[40,33,128]{2,1,0:T(8,128)}, u32[]{:S(2)}) %copy-start.1) | copy-done | bytes 675864 | tf_op jit(solution)/shard_map/cond
  63.8 0.2 copy-done.2
  64.0 2.9 %multiply_add_fusion.39 = (f32[40,32,128]{2,1,0:T(8,128)S(1)}, f32[40,32,128]{2,1,0:T(8,128)S(1)}) fusion(f32[40,34,129]{2,1,0:T(8,128)} %copy.55, f32[40,34,129]{2,1,0:T(8,128)} %copy.54, f32[40,33,128]{2,1,0:T(8,128)S(1)} %copy-done.1, f32[40,33,128]{2,1,0:T(8,128)S(1)} %copy-done.2, f32[32,128]{1,0:T(8,128)S(1)} %get-tuple-element.154, ...), kind=kLoop, calls=%fused_computation.362 | loop fusion | flops 2621440 | bytes 4603904 | tf_op jit(solution)/shard_map/cond/branch_1_fun/add | solution.py:42
  67.1 0.4 fusion.169
  67.5 0.2 constant_dynamic-update-slice_fusion.79
  68.4 7.2 %all_gather.7 = f32[4,32,128]{2,1,0:T(8,128)S(1)} all-gather(f32[1,32,128]{2,1,0:T(8,128)S(1)} %get-tuple-element.167), channel_id=1, replica_groups=mesh['sec'=4,'gx'=4,'gy'=2] {'sec'}, dimensions={0}, use_global_device_ids=true | all-gather | bytes 81920 | tf_op jit(solution)/shard_map/all_gather | solution.py:146
  75.7 4.5 %collective-permute-start.12 = (f32[5,3,4,128]{3,2,1,0:T(4,128)S(1)}, f32[5,3,4,128]{3,2,1,0:T(4,128)S(1)}, u32[]{:S(2)}, u32[]{:S(2)}) collective-permute-start(f32[5,3,4,128]{3,2,1,0:T(4,128)S(1)} %get-tuple-element.455), channel_id=1, source_target_pairs={{0,2},{2,4},{4,6},{1,3},{3,5},{5,7},{8,10},{10,12},{12,14},{9,11},... | collective-permute-start | bytes 92168 | tf_op jit(solution)/shard_map/ppermute | solution.py:22
  80.2 1.3 %collective-permute-start.13 = (f32[5,3,4,128]{3,2,1,0:T(4,128)S(1)}, f32[5,3,4,128]{3,2,1,0:T(4,128)S(1)}, u32[]{:S(2)}, u32[]{:S(2)}) collective-permute-start(f32[5,3,4,128]{3,2,1,0:T(4,128)S(1)} %get-tuple-element.456), channel_id=1, source_target_pairs={{2,0},{4,2},{6,4},{3,1},{5,3},{7,5},{10,8},{12,10},{14,12},{11,9},... | collective-permute-start | bytes 92168 | tf_op jit(solution)/shard_map/ppermute | solution.py:24
  81.5 0.3 collective-permute-done.12
  81.8 4.2 %collective-permute-done.13 = f32[5,3,4,128]{3,2,1,0:T(4,128)S(1)} collective-permute-done((f32[5,3,4,128]{3,2,1,0:T(4,128)S(1)}, f32[5,3,4,128]{3,2,1,0:T(4,128)S(1)}, u32[]{:S(2)}, u32[]{:S(2)}) %collective-permute-start.13) | collective-permute-done | bytes 30752 | tf_op jit(solution)/shard_map/ppermute | solution.py:24
  86.1 0.1 fusion.591
  86.2 1.3 %collective-permute-start.14 = (f32[5,3,40,4]{3,2,1,0:T(8,128)S(1)}, f32[5,3,40,4]{3,2,1,0:T(8,128)S(1)}, u32[]{:S(2)}, u32[]{:S(2)}) collective-permute-start(f32[5,3,40,4]{3,2,1,0:T(8,128)S(1)} %get-tuple-element.451), channel_id=1, source_target_pairs={{0,1},{2,3},{4,5},{6,7},{8,9},{10,11},{12,13},{14,15},{16,17},{18,... | collective-permute-start | bytes 28808 | tf_op jit(solution)/shard_map/ppermute | solution.py:22
  87.5 1.3 %collective-permute-start.15 = (f32[5,3,40,4]{3,2,1,0:T(8,128)S(1)}, f32[5,3,40,4]{3,2,1,0:T(8,128)S(1)}, u32[]{:S(2)}, u32[]{:S(2)}) collective-permute-start(f32[5,3,40,4]{3,2,1,0:T(8,128)S(1)} %get-tuple-element.452), channel_id=1, source_target_pairs={{1,0},{3,2},{5,4},{7,6},{9,8},{11,10},{13,12},{15,14},{17,16},{19,... | collective-permute-start | bytes 28808 | tf_op jit(solution)/shard_map/ppermute | solution.py:24
  88.9 2.2 %collective-permute-done.15 = f32[5,3,40,4]{3,2,1,0:T(8,128)S(1)} collective-permute-done((f32[5,3,40,4]{3,2,1,0:T(8,128)S(1)}, f32[5,3,40,4]{3,2,1,0:T(8,128)S(1)}, u32[]{:S(2)}, u32[]{:S(2)}) %collective-permute-start.15) | collective-permute-done | bytes 9632 | tf_op jit(solution)/shard_map/ppermute | solution.py:24
  91.0 0.4 pad_maximum_fusion.6
  91.5 0.4 fusion.347
  91.9 0.4 fusion.334
  92.3 0.4 fusion.321
  92.7 0.2 fusion.413
  93.0 0.6 fusion.436
  (139 shorter events, 1.6 us)
Async XLA Ops:
  0.0 9.3 %collective-permute-start = (f32[40,1,128]{2,0,1:T(8,128)S(1)}, f32[40,1,128]{2,0,1:T(8,128)S(1)}, u32[]{:S(2)}, u32[]{:S(2)}) collective-permute-start(f32[40,1,128]{2,0,1:T(8,128)S(1)} %broadcast.6507), channel_id=1, source_target_pairs={{2,0},{4,2},{6,4},{3,1},{5,3},{7,5},{10,8},{12,10},{14,12},{11,9},... | collective-permute-start | bytes 61448 | tf_op jit(solution)/shard_map/ppermute | solution.py:24
  1.3 8.0 %collective-permute-start.1 = (f32[40,1,128]{2,0,1:T(8,128)S(1)}, f32[40,1,128]{2,0,1:T(8,128)S(1)}, u32[]{:S(2)}, u32[]{:S(2)}) collective-permute-start(f32[40,1,128]{2,0,1:T(8,128)S(1)} %broadcast.6507), channel_id=1, source_target_pairs={{0,2},{2,4},{4,6},{1,3},{3,5},{5,7},{8,10},{10,12},{12,14},{9,11},... | collective-permute-start | bytes 61448 | tf_op jit(solution)/shard_map/ppermute | solution.py:22
  9.9 5.4 %collective-permute-start.2 = (f32[40,34,1]{0,2,1:T(1,128)S(1)}, f32[40,34,1]{0,2,1:T(1,128)S(1)}, u32[]{:S(2)}, u32[]{:S(2)}) collective-permute-start(f32[40,34,1]{0,2,1:T(1,128)S(1)} %copy.56), channel_id=1, source_target_pairs={{1,0},{3,2},{5,4},{7,6},{9,8},{11,10},{13,12},{15,14},{17,16},{19,... | collective-permute-start | bytes 16328 | tf_op jit(solution)/shard_map/ppermute | solution.py:24
  11.5 4.1 %collective-permute-start.3 = (f32[40,34,1]{0,2,1:T(1,128)S(1)}, f32[40,34,1]{0,2,1:T(1,128)S(1)}, u32[]{:S(2)}, u32[]{:S(2)}) collective-permute-start(f32[40,34,1]{0,2,1:T(1,128)S(1)} %copy.57), channel_id=1, source_target_pairs={{0,1},{2,3},{4,5},{6,7},{8,9},{10,11},{12,13},{14,15},{16,17},{18,... | collective-permute-start | bytes 16328 | tf_op jit(solution)/shard_map/ppermute | solution.py:22
  20.0 15.3 %copy-start.5 = (f32[3,32,128]{2,1,0:T(8,128)S(1)}, f32[3,32,128]{2,1,0:T(8,128)}, u32[]{:S(2)}) copy-start(f32[3,32,128]{2,1,0:T(8,128)} %param.20) | copy-start | bytes 147460
  20.0 15.3 %copy-start.4 = (f32[3,32,128]{2,1,0:T(8,128)S(1)}, f32[3,32,128]{2,1,0:T(8,128)}, u32[]{:S(2)}) copy-start(f32[3,32,128]{2,1,0:T(8,128)} %param.21) | copy-start | bytes 147460
  20.1 15.3 %copy-start.6 = (f32[3,32,128]{2,1,0:T(8,128)S(1)}, f32[3,32,128]{2,1,0:T(8,128)}, u32[]{:S(2)}) copy-start(f32[3,32,128]{2,1,0:T(8,128)} %param.19) | copy-start | bytes 147460
  20.7 19.5 %collective-permute-start.4 = (f32[40,1,128]{0,2,1:T(8,128)S(1)}, f32[40,1,128]{0,2,1:T(8,128)S(1)}, u32[]{:S(2)}, u32[]{:S(2)}) collective-permute-start(f32[40,1,128]{0,2,1:T(8,128)S(1)} %get-tuple-element.434), channel_id=1, source_target_pairs={{2,0},{4,2},{6,4},{3,1},{5,3},{7,5},{10,8},{12,10},{14,12},{11,9},... | collective-permute-start | bytes 61448 | tf_op jit(solution)/shard_map/ppermute | solution.py:24
  22.0 18.2 %collective-permute-start.5 = (f32[40,1,128]{0,2,1:T(8,128)S(1)}, f32[40,1,128]{0,2,1:T(8,128)S(1)}, u32[]{:S(2)}, u32[]{:S(2)}) collective-permute-start(f32[40,1,128]{0,2,1:T(8,128)S(1)} %get-tuple-element.433), channel_id=1, source_target_pairs={{0,2},{2,4},{4,6},{1,3},{3,5},{5,7},{8,10},{10,12},{12,14},{9,11},... | collective-permute-start | bytes 61448 | tf_op jit(solution)/shard_map/ppermute | solution.py:22
  35.4 11.9 %collective-permute-start.8 = (f32[5,3,4,128]{3,2,1,0:T(4,128)S(1)}, f32[5,3,4,128]{3,2,1,0:T(4,128)S(1)}, u32[]{:S(2)}, u32[]{:S(2)}) collective-permute-start(f32[5,3,4,128]{3,2,1,0:T(4,128)S(1)} %get-tuple-element.457), channel_id=1, source_target_pairs={{0,2},{2,4},{4,6},{1,3},{3,5},{5,7},{8,10},{10,12},{12,14},{9,11},... | collective-permute-start | bytes 92168 | tf_op jit(solution)/shard_map/ppermute | solution.py:22
  39.0 8.4 %collective-permute-start.9 = (f32[5,3,4,128]{3,2,1,0:T(4,128)S(1)}, f32[5,3,4,128]{3,2,1,0:T(4,128)S(1)}, u32[]{:S(2)}, u32[]{:S(2)}) collective-permute-start(f32[5,3,4,128]{3,2,1,0:T(4,128)S(1)} %get-tuple-element.458), channel_id=1, source_target_pairs={{2,0},{4,2},{6,4},{3,1},{5,3},{7,5},{10,8},{12,10},{14,12},{11,9},... | collective-permute-start | bytes 92168 | tf_op jit(solution)/shard_map/ppermute | solution.py:24
  40.9 9.2 %collective-permute-start.6 = (f32[40,34,1]{0,2,1:T(1,128)}, f32[40,34,1]{0,2,1:T(1,128)S(1)}, u32[]{:S(2)}, u32[]{:S(2)}) collective-permute-start(f32[40,34,1]{0,2,1:T(1,128)} %get-tuple-element.432), channel_id=1, source_target_pairs={{1,0},{3,2},{5,4},{7,6},{9,8},{11,10},{13,12},{15,14},{17,16},{19,... | collective-permute-start | bytes 16328 | tf_op jit(solution)/shard_map/ppermute | solution.py:24
  42.2 7.9 %collective-permute-start.7 = (f32[40,34,1]{0,2,1:T(1,128)}, f32[40,34,1]{0,2,1:T(1,128)}, u32[]{:S(2)}, u32[]{:S(2)}) collective-permute-start(f32[40,34,1]{0,2,1:T(1,128)} %get-tuple-element.431), channel_id=1, source_target_pairs={{0,1},{2,3},{4,5},{6,7},{8,9},{10,11},{12,13},{14,15},{16,17},{18,... | collective-permute-start | bytes 16328 | tf_op jit(solution)/shard_map/ppermute | solution.py:22
  47.5 5.9 %collective-permute-start.10 = (f32[5,3,40,4]{3,2,1,0:T(8,128)S(1)}, f32[5,3,40,4]{3,2,1,0:T(8,128)S(1)}, u32[]{:S(2)}, u32[]{:S(2)}) collective-permute-start(f32[5,3,40,4]{3,2,1,0:T(8,128)S(1)} %get-tuple-element.453), channel_id=1, source_target_pairs={{0,1},{2,3},{4,5},{6,7},{8,9},{10,11},{12,13},{14,15},{16,17},{18,... | collective-permute-start | bytes 28808 | tf_op jit(solution)/shard_map/ppermute | solution.py:22
  48.8 4.6 %collective-permute-start.11 = (f32[5,3,40,4]{3,2,1,0:T(8,128)S(1)}, f32[5,3,40,4]{3,2,1,0:T(8,128)S(1)}, u32[]{:S(2)}, u32[]{:S(2)}) collective-permute-start(f32[5,3,40,4]{3,2,1,0:T(8,128)S(1)} %get-tuple-element.454), channel_id=1, source_target_pairs={{1,0},{3,2},{5,4},{7,6},{9,8},{11,10},{13,12},{15,14},{17,16},{19,... | collective-permute-start | bytes 28808 | tf_op jit(solution)/shard_map/ppermute | solution.py:24
  54.2 0.9 copy-start.3
  54.3 0.9 copy-start.7
  54.3 1.7 %copy-start = (f32[40,34,129]{0,2,1:T(8,128)S(1)}, f32[40,34,129]{0,2,1:T(8,128)}, u32[]{:S(2)}) copy-start(f32[40,34,129]{0,2,1:T(8,128)} %get-tuple-element.429) | copy-start | bytes 2105284
  62.6 1.1 %copy-start.1 = (f32[40,33,128]{2,1,0:T(8,128)S(1)}, f32[40,33,128]{2,1,0:T(8,128)}, u32[]{:S(2)}) copy-start(f32[40,33,128]{2,1,0:T(8,128)} %get-tuple-element.158) | copy-start | bytes 2027524 | tf_op jit(solution)/shard_map/cond
  62.6 1.4 %copy-start.2 = (f32[40,33,128]{2,1,0:T(8,128)S(1)}, f32[40,33,128]{2,1,0:T(8,128)}, u32[]{:S(2)}) copy-start(f32[40,33,128]{2,1,0:T(8,128)} %get-tuple-element.157) | copy-start | bytes 2027524 | tf_op jit(solution)/shard_map/cond
  75.7 6.1 %collective-permute-start.12 = (f32[5,3,4,128]{3,2,1,0:T(4,128)S(1)}, f32[5,3,4,128]{3,2,1,0:T(4,128)S(1)}, u32[]{:S(2)}, u32[]{:S(2)}) collective-permute-start(f32[5,3,4,128]{3,2,1,0:T(4,128)S(1)} %get-tuple-element.455), channel_id=1, source_target_pairs={{0,2},{2,4},{4,6},{1,3},{3,5},{5,7},{8,10},{10,12},{12,14},{9,11},... | collective-permute-start | bytes 92168 | tf_op jit(solution)/shard_map/ppermute | solution.py:22
  80.2 5.8 %collective-permute-start.13 = (f32[5,3,4,128]{3,2,1,0:T(4,128)S(1)}, f32[5,3,4,128]{3,2,1,0:T(4,128)S(1)}, u32[]{:S(2)}, u32[]{:S(2)}) collective-permute-start(f32[5,3,4,128]{3,2,1,0:T(4,128)S(1)} %get-tuple-element.456), channel_id=1, source_target_pairs={{2,0},{4,2},{6,4},{3,1},{5,3},{7,5},{10,8},{12,10},{14,12},{11,9},... | collective-permute-start | bytes 92168 | tf_op jit(solution)/shard_map/ppermute | solution.py:24
  86.2 2.6 %collective-permute-start.14 = (f32[5,3,40,4]{3,2,1,0:T(8,128)S(1)}, f32[5,3,40,4]{3,2,1,0:T(8,128)S(1)}, u32[]{:S(2)}, u32[]{:S(2)}) collective-permute-start(f32[5,3,40,4]{3,2,1,0:T(8,128)S(1)} %get-tuple-element.451), channel_id=1, source_target_pairs={{0,1},{2,3},{4,5},{6,7},{8,9},{10,11},{12,13},{14,15},{16,17},{18,... | collective-permute-start | bytes 28808 | tf_op jit(solution)/shard_map/ppermute | solution.py:22
  87.5 3.5 %collective-permute-start.15 = (f32[5,3,40,4]{3,2,1,0:T(8,128)S(1)}, f32[5,3,40,4]{3,2,1,0:T(8,128)S(1)}, u32[]{:S(2)}, u32[]{:S(2)}) collective-permute-start(f32[5,3,40,4]{3,2,1,0:T(8,128)S(1)} %get-tuple-element.452), channel_id=1, source_target_pairs={{1,0},{3,2},{5,4},{7,6},{9,8},{11,10},{13,12},{15,14},{17,16},{19,... | collective-permute-start | bytes 28808 | tf_op jit(solution)/shard_map/ppermute | solution.py:24
where the time goes:
time: 94.5 us; the launch traced here: 93.6 us
  starting transfers between devices  37.9 us (40%)
  other arithmetic  18.1 us (19%)
  blocking collectives  15.9 us (17%)
  local copies, waits for them, and re-layouts  13.9 us (15%)
  waiting for transfers between devices  6.69 us (7%)
    ppermute x8, starting transfers between devices, extended(): lax.ppermute(tail, axis, [(i, (i + 1) % count) for i in range(ends)])  27.5 us
    all_gather x2, blocking collectives, on_device(): basal_rows = lax.all_gather(velocity[:1], 'sec', axis=0, tiled=True)  15.9 us
    ppermute x8, starting transfers between devices, extended(): lax.ppermute(head, axis, [((i + 1) % count, i) for i in range(ends)])  10.3 us
    another operation x7, local copies, waits for them, and re-layouts  7.61 us
    concatenate x9, other arithmetic, extended(): jnp.concatenate([lax.ppermute(tail, axis, [(i, (i + 1) % count) for i in...  6.56 us
    ppermute x8, waiting for transfers between devices, extended(): lax.ppermute(head, axis, [((i + 1) % count, i) for i in range(ends)])  6.41 us
    add x2, other arithmetic, ice_core(): right_side = driving + viscous * (x_plus + x_minus + y_plus + y_minus)  4.17 us
    select_n x7, other arithmetic, sweep_padded(): jnp.where(inside > 0.5, numerator / (denominator + (1.0 - inside)), 0.0)  2.73 us
  transfers between devices with their start and end apart: 16, of which 3 were waited for; matrix products, arithmetic and copies ran while one was open for 10% of the time, Pallas kernels for 0%

commit v1 on v0

--- a/solution.py
+++ b/solution.py
@@ -9,6 +9,23 @@
 VERT = 4.0
 FLOOR = 0.25
 HEATING = 0.5
+
+
+def in_order(blocks, dim):
+    dims = list(blocks.shape[1:])
+    dims[dim] *= blocks.shape[0]
+    return jnp.moveaxis(blocks, 0, dim).reshape(dims)
+
+
+def gather_around(value, axis, dim):
+    peers = lax.axis_size(axis)
+    ahead = [(i, (i + 1) % peers) for i in range(peers)]
+    blocks = [value]
+    while len(blocks) < peers:
+        blocks.append(lax.ppermute(blocks[-1], axis, ahead))
+    index = lax.axis_index(axis)
+    blocks = jnp.stack(blocks)[(index - jnp.arange(peers)) % peers]
+    return in_order(blocks, dim)
 
 
 def extended(cells, sides, width):
@@ -143,7 +160,7 @@
             ),
             lambda: jnp.zeros_like(old_velocity),
         )
-        basal_rows = lax.all_gather(velocity[:1], "sec", axis=0, tiled=True)
+        basal_rows = gather_around(velocity[:1], "sec", 0)
         sliding = basal_rows[:sectors]
         squared = sliding * sliding
         trans_eff = transmissivity * (1.0 + squared / (1.0 + squared))

time: 94.5 us -> 108 us (1.14)
  waiting for transfers between devices: 6.69 us -> 26.8 us
  blocking collectives: 15.9 us -> 0 us
  starting transfers between devices: 37.9 us -> 42.3 us
  local copies, waits for them, and re-layouts: 13.9 us -> 17.1 us
  other arithmetic: 18.1 us -> 19.6 us
    ppermute x0 -> x6, waiting for transfers between devices: none -> 16.4 us  [gather_around(): blocks.append(lax.ppermute(blocks[-1], axis, ahead))]
    all_gather x2 -> x0, blocking collectives: 15.9 us -> none  [on_device(): basal_rows = lax.all_gather(velocity[:1], 'sec', axis=0, tiled=True)]
    ppermute x0 -> x6, starting transfers between devices: none -> 4.98 us  [gather_around(): blocks.append(lax.ppermute(blocks[-1], axis, ahead))]
    ppermute x8, waiting for transfers between devices: 6.41 us -> 9.58 us  [extended(): lax.ppermute(head, axis, [((i + 1) % count, i) for i in range(ends)])]
    gather x0 -> x2, local copies, waits for them, and re-layouts: none -> 1.22 us  [gather_around(): blocks = jnp.stack(blocks)[(index - jnp.arange(peers)) % peers]]
    cond x42 -> x43, local copies, waits for them, and re-layouts: 1.47 us -> 2.19 us
    another operation x7 -> x8, local copies, waits for them, and re-layouts: 7.61 us -> 8.23 us
  transfers between devices with their start and end apart: 16 -> 22, of which waited for: 3 -> 9; matrix products, arithmetic and copies ran while one was open for 10% -> 10% of each run, Pallas kernels for 0% -> 0%
where the time goes in v1:
time: 108 us; the launch traced here: 107 us
  starting transfers between devices  42.3 us (39%)
  waiting for transfers between devices  26.8 us (25%)
  other arithmetic  19.6 us (18%)
  local copies, waits for them, and re-layouts  17.1 us (16%)
    ppermute x8, starting transfers between devices, extended(): lax.ppermute(tail, axis, [(i, (i + 1) % count) for i in range(ends)])  27 us
    ppermute x6, waiting for transfers between devices, gather_around(): blocks.append(lax.ppermute(blocks[-1], axis, ahead))  16.4 us
    ppermute x8, starting transfers between devices, extended(): lax.ppermute(head, axis, [((i + 1) % count, i) for i in range(ends)])  10.3 us
    ppermute x8, waiting for transfers between devices, extended(): lax.ppermute(head, axis, [((i + 1) % count, i) for i in range(ends)])  9.58 us
    another operation x7, local copies, waits for them, and re-layouts  7.63 us
    concatenate x9, other arithmetic, extended(): jnp.concatenate([lax.ppermute(tail, axis, [(i, (i + 1) % count) for i in...  6.56 us
    ppermute x6, starting transfers between devices, gather_around(): blocks.append(lax.ppermute(blocks[-1], axis, ahead))  4.98 us
    add x2, other arithmetic, ice_core(): right_side = driving + viscous * (x_plus + x_minus + y_plus + y_minus)  4.17 us
  transfers between devices with their start and end apart: 22, of which 9 were waited for; matrix products, arithmetic and copies ran while one was open for 10% of the time, Pallas kernels for 0%

profile of v1, /device:TPU:0, one launch (start us, length us, event | category | flops | bytes accessed | tf_op | source)
XLA Modules:
  0.0 107.0 jit_solution(3042547285374319777)
XLA Ops:
  0.0 1.3 %collective-permute-start = (f32[40,1,128]{2,0,1:T(8,128)S(1)}, f32[40,1,128]{2,0,1:T(8,128)S(1)}, u32[]{:S(2)}, u32[]{:S(2)}) collective-permute-start(f32[40,1,128]{2,0,1:T(8,128)S(1)} %broadcast.6575), channel_id=1, source_target_pairs={{2,0},{4,2},{6,4},{3,1},{5,3},{7,5},{10,8},{12,10},{14,12},{11,9},... | collective-permute-start | bytes 61448 | tf_op jit(solution)/shard_map/ppermute | solution.py:41
  1.3 5.6 %collective-permute-start.1 = (f32[40,1,128]{2,0,1:T(8,128)S(1)}, f32[40,1,128]{2,0,1:T(8,128)S(1)}, u32[]{:S(2)}, u32[]{:S(2)}) collective-permute-start(f32[40,1,128]{2,0,1:T(8,128)S(1)} %broadcast.6575), channel_id=1, source_target_pairs={{0,2},{2,4},{4,6},{1,3},{3,5},{5,7},{8,10},{10,12},{12,14},{9,11},... | collective-permute-start | bytes 61448 | tf_op jit(solution)/shard_map/ppermute | solution.py:39
  6.9 0.8 bitcast_dynamic-update-slice_fusion.5
  7.7 0.8 convert_multiply_fusion
  8.5 0.7 dynamic-slice_bitcast_fusion
  9.3 0.7 convert_bitcast_fusion
  10.6 1.3 %collective-permute-start.2 = (f32[40,34,1]{0,2,1:T(1,128)S(1)}, f32[40,34,1]{0,2,1:T(1,128)S(1)}, u32[]{:S(2)}, u32[]{:S(2)}) collective-permute-start(f32[40,34,1]{0,2,1:T(1,128)S(1)} %copy.56), channel_id=1, source_target_pairs={{1,0},{3,2},{5,4},{7,6},{9,8},{11,10},{13,12},{15,14},{17,16},{19,... | collective-permute-start | bytes 16328 | tf_op jit(solution)/shard_map/ppermute | solution.py:41
  12.2 3.0 %collective-permute-start.3 = (f32[40,34,1]{0,2,1:T(1,128)S(1)}, f32[40,34,1]{0,2,1:T(1,128)S(1)}, u32[]{:S(2)}, u32[]{:S(2)}) collective-permute-start(f32[40,34,1]{0,2,1:T(1,128)S(1)} %copy.57), channel_id=1, source_target_pairs={{0,1},{2,3},{4,5},{6,7},{8,9},{10,11},{12,13},{14,15},{16,17},{18,... | collective-permute-start | bytes 16328 | tf_op jit(solution)/shard_map/ppermute | solution.py:39
  15.6 0.5 collective-permute-done.3
  16.4 0.4 maximum_maximum_fusion.1
  16.9 3.6 %conditional.2 = (f32[40,32,128]{2,1,0:T(8,128)S(1)}) conditional(s32[]{:T(128)} %convert_element_type.13, () %tuple.32, (f32[32,128]{1,0:T(8,128)S(1)}, f32[32,128]{1,0:T(8,128)S(1)}, f32[40,1,128]{2,0,1:T(8,128)S(1)}, f32[40,1,128]{2,0,1:T(8,128)S(1)}, f32[40,34,129]{2,0,1:T(8,128)S(1)}, /*index=5*/f32[40,34,129]{2,0,1:T(8,128)S(1)}, ...), branch_computations={%region_0.1_spmd, %region_1.2_spmd} | conditional | flops 5099559 | bytes 16611208 | solution.py:148
  16.9 0.5 copy.47
  17.4 0.5 copy.48
  17.8 1.2 %multiply_add_fusion = (f32[40,32,128]{2,1,0:T(8,128)S(1)}, f32[40,32,128]{2,1,0:T(8,128)S(1)}) fusion(f32[40,34,129]{2,1,0:T(8,128)S(1)} %copy.48, f32[40,34,129]{2,1,0:T(8,128)S(1)} %copy.47, f32[40,1,128]{2,1,0:T(1,128)S(1)} %bitcast.64, f32[40,1,128]{2,1,0:T(1,128)S(1)} %bitcast.65, f32[32,128]{1,0:T(8,128)S(1)} %get-tuple-element.148, ...), kind=kLoop, calls=%fused_computation.4 | loop fusion | flops 2457600 | bytes 2695328 | tf_op jit(solution)/shard_map/cond/branch_1_fun/add | solution.py:59
  19.3 0.4 fusion.11
  20.5 0.6 copy.49
  21.2 0.6 slice_bitcast_fusion.10
  21.8 1.9 %collective-permute-start.8 = (f32[1,32,128]{2,1,0:T(8,128)S(1)}, f32[1,32,128]{2,1,0:T(8,128)S(1)}, u32[]{:S(2)}, u32[]{:S(2)}) collective-permute-start(f32[1,32,128]{2,1,0:T(8,128)S(1)} %get-tuple-element.447), channel_id=1, source_target_pairs={{0,8},{8,16},{16,24},{24,0},{1,9},{9,17},{17,25},{25,1},{2,10},{10... | collective-permute-start | bytes 49160 | tf_op jit(solution)/shard_map/ppermute | solution.py:25
  23.7 1.3 %collective-permute-start.4 = (f32[40,1,128]{0,2,1:T(8,128)S(1)}, f32[40,1,128]{0,2,1:T(8,128)S(1)}, u32[]{:S(2)}, u32[]{:S(2)}) collective-permute-start(f32[40,1,128]{0,2,1:T(8,128)S(1)} %get-tuple-element.439), channel_id=1, source_target_pairs={{2,0},{4,2},{6,4},{3,1},{5,3},{7,5},{10,8},{12,10},{14,12},{11,9},... | collective-permute-start | bytes 61448 | tf_op jit(solution)/shard_map/ppermute | solution.py:41
  25.0 4.5 %collective-permute-start.5 = (f32[40,1,128]{0,2,1:T(8,128)S(1)}, f32[40,1,128]{0,2,1:T(8,128)S(1)}, u32[]{:S(2)}, u32[]{:S(2)}) collective-permute-start(f32[40,1,128]{0,2,1:T(8,128)S(1)} %get-tuple-element.438), channel_id=1, source_target_pairs={{0,2},{2,4},{4,6},{1,3},{3,5},{5,7},{8,10},{10,12},{12,14},{9,11},... | collective-permute-start | bytes 61448 | tf_op jit(solution)/shard_map/ppermute | solution.py:39
  29.6 1.5 %collective-permute-start.9 = (f32[1,32,128]{2,1,0:T(8,128)S(1)}, f32[1,32,128]{2,1,0:T(8,128)}, u32[]{:S(2)}, u32[]{:S(2)}) collective-permute-start(f32[1,32,128]{2,1,0:T(8,128)S(1)} %collective-permute-done.8), channel_id=1, source_target_pairs={{0,8},{8,16},{16,24},{24,0},{1,9},{9,17},{17,25},{25,1},{2,10},{10... | collective-permute-start | bytes 49160 | tf_op jit(solution)/shard_map/ppermute | solution.py:25
  31.2 3.2 %collective-permute-done.9 = f32[1,32,128]{2,1,0:T(8,128)} collective-permute-done((f32[1,32,128]{2,1,0:T(8,128)S(1)}, f32[1,32,128]{2,1,0:T(8,128)}, u32[]{:S(2)}, u32[]{:S(2)}) %collective-permute-start.9) | collective-permute-done | bytes 16416 | tf_op jit(solution)/shard_map/ppermute | solution.py:25
  34.4 0.6 collective-permute-start.10
  35.0 0.6 pad_maximum_fusion.9
  35.7 1.3 %collective-permute-start.6 = (f32[40,34,1]{0,2,1:T(1,128)}, f32[40,34,1]{0,2,1:T(1,128)}, u32[]{:S(2)}, u32[]{:S(2)}) collective-permute-start(f32[40,34,1]{0,2,1:T(1,128)} %get-tuple-element.437), channel_id=1, source_target_pairs={{1,0},{3,2},{5,4},{7,6},{9,8},{11,10},{13,12},{15,14},{17,16},{19,... | collective-permute-start | bytes 16328 | tf_op jit(solution)/shard_map/ppermute | solution.py:41
  37.0 4.2 %collective-permute-start.7 = (f32[40,34,1]{0,2,1:T(1,128)}, f32[40,34,1]{0,2,1:T(1,128)}, u32[]{:S(2)}, u32[]{:S(2)}) collective-permute-start(f32[40,34,1]{0,2,1:T(1,128)} %get-tuple-element.436), channel_id=1, source_target_pairs={{0,1},{2,3},{4,5},{6,7},{8,9},{10,11},{12,13},{14,15},{16,17},{18,... | collective-permute-start | bytes 16328 | tf_op jit(solution)/shard_map/ppermute | solution.py:39
  41.3 0.8 maximum_bitcast_fusion
  42.1 0.6 gather_fusion
  42.8 3.5 %collective-permute-start.11 = (f32[5,3,4,128]{3,2,1,0:T(4,128)S(1)}, f32[5,3,4,128]{3,2,1,0:T(4,128)S(1)}, u32[]{:S(2)}, u32[]{:S(2)}) collective-permute-start(f32[5,3,4,128]{3,2,1,0:T(4,128)S(1)} %get-tuple-element.464), channel_id=1, source_target_pairs={{0,2},{2,4},{4,6},{1,3},{3,5},{5,7},{8,10},{10,12},{12,14},{9,11},... | collective-permute-start | bytes 92168 | tf_op jit(solution)/shard_map/ppermute | solution.py:39
  46.3 1.3 %collective-permute-start.12 = (f32[5,3,4,128]{3,2,1,0:T(4,128)S(1)}, f32[5,3,4,128]{3,2,1,0:T(4,128)S(1)}, u32[]{:S(2)}, u32[]{:S(2)}) collective-permute-start(f32[5,3,4,128]{3,2,1,0:T(4,128)S(1)} %get-tuple-element.465), channel_id=1, source_target_pairs={{2,0},{4,2},{6,4},{3,1},{5,3},{7,5},{10,8},{12,10},{14,12},{11,9},... | collective-permute-start | bytes 92168 | tf_op jit(solution)/shard_map/ppermute | solution.py:41
  47.6 1.3 %pad_maximum_fusion.3 = (f32[40,33,128]{2,1,0:T(8,128)}, f32[40,33,128]{2,1,0:T(8,128)}) fusion(f32[40,32,128]{2,1,0:T(8,128)S(1)} %get-tuple-element.474, f32[40,1,128]{2,1,0:T(1,128)S(1)} %copy.52, f32[40,1,128]{2,1,0:T(1,128)S(1)} %copy.50), kind=kLoop, calls=%fused_computation.729 | loop fusion | flops 337920 | bytes 2048000 | tf_op jit(solution)/shard_map/concatenate | solution.py:37
  48.9 3.2 %collective-permute-done.12 = f32[5,3,4,128]{3,2,1,0:T(4,128)S(1)} collective-permute-done((f32[5,3,4,128]{3,2,1,0:T(4,128)S(1)}, f32[5,3,4,128]{3,2,1,0:T(4,128)S(1)}, u32[]{:S(2)}, u32[]{:S(2)}) %collective-permute-start.12) | collective-permute-done | bytes 30752 | tf_op jit(solution)/shard_map/ppermute | solution.py:41
  52.3 1.3 %collective-permute-start.13 = (f32[5,3,40,4]{3,2,1,0:T(8,128)S(1)}, f32[5,3,40,4]{3,2,1,0:T(8,128)S(1)}, u32[]{:S(2)}, u32[]{:S(2)}) collective-permute-start(f32[5,3,40,4]{3,2,1,0:T(8,128)S(1)} %get-tuple-element.460), channel_id=1, source_target_pairs={{0,1},{2,3},{4,5},{6,7},{8,9},{10,11},{12,13},{14,15},{16,17},{18,... | collective-permute-start | bytes 28808 | tf_op jit(solution)/shard_map/ppermute | solution.py:39
  53.6 1.3 %collective-permute-start.14 = (f32[5,3,40,4]{3,2,1,0:T(8,128)S(1)}, f32[5,3,40,4]{3,2,1,0:T(8,128)S(1)}, u32[]{:S(2)}, u32[]{:S(2)}) collective-permute-start(f32[5,3,40,4]{3,2,1,0:T(8,128)S(1)} %get-tuple-element.461), channel_id=1, source_target_pairs={{1,0},{3,2},{5,4},{7,6},{9,8},{11,10},{13,12},{15,14},{17,16},{19,... | collective-permute-start | bytes 28808 | tf_op jit(solution)/shard_map/ppermute | solution.py:41
  54.9 3.3 %maximum_maximum_fusion = (f32[40,34,129]{0,2,1:T(8,128)}, f32[40,34,129]{0,2,1:T(8,128)}) fusion(f32[40,1,128]{0,2,1:T(8,128)S(1)} %collective-permute-done.4, f32[40,32,128]{0,2,1:T(8,128)S(1)} %copy.49, f32[40,1,128]{0,2,1:T(8,128)S(1)} %collective-permute-done.5, f32[40,34,1]{0,2,1:T(1,128)} %collective-permute-done.7, ...), kind=kLoop, calls=%fused_computation.725 | loop fusion | flops 1052640 | bytes 2110720 | tf_op jit(solution)/shard_map/concatenate | solution.py:37
  58.2 0.4 pad_maximum_fusion.5
  58.6 0.4 fusion.389
  59.1 0.4 fusion.376
  59.5 0.4 fusion.363
  60.2 0.6 copy-done
  60.8 13.7 %conditional.3 = (f32[1,32,128]{2,1,0:T(8,128)S(1)}, f32[1,32,128]{2,1,0:T(8,128)}, f32[1,1,32,128]{3,2,1,0:T(8,128)S(1)}) conditional(s32[]{:T(128)} %convert_element_type.13, () %tuple.31, (f32[32,128]{1,0:T(8,128)S(1)}, f32[32,128]{1,0:T(8,128)S(1)}, f32[40,32,128]{2,1,0:T(8,128)S(1)}, f32[40,33,128]{2,1,0:T(8,128)}, f32[40,33,128]{2,1,0:T(8,128)}, ...), branch_computations={%region_2.3_spmd, %region_3.4_spmd} | conditional | flops 5423103 | bytes 25941332 | solution.py:148
  60.8 4.1 %copy.54 = f32[40,34,129]{2,1,0:T(8,128)} copy(f32[40,34,129]{0,2,1:T(8,128)} %get-tuple-element.225) | data formatting | bytes 1403520 | tf_op jit(solution)/shard_map
  64.8 2.6 %copy.55 = f32[40,34,129]{2,1,0:T(8,128)} copy(f32[40,34,129]{0,2,1:T(8,128)S(1)} %get-tuple-element.226) | data formatting | bytes 1403520 | tf_op jit(solution)/shard_map
  67.5 1.1 %copy-done.1 = f32[40,33,128]{2,1,0:T(8,128)S(1)} copy-done((f32[40,33,128]{2,1,0:T(8,128)S(1)}, f32[40,33,128]{2,1,0:T(8,128)}, u32[]{:S(2)}) %copy-start.1) | copy-done | bytes 675864 | tf_op jit(solution)/shard_map/cond
  68.8 2.9 %multiply_add_fusion.39 = (f32[40,32,128]{2,1,0:T(8,128)S(1)}, f32[40,32,128]{2,1,0:T(8,128)S(1)}) fusion(f32[40,34,129]{2,1,0:T(8,128)} %copy.55, f32[40,34,129]{2,1,0:T(8,128)} %copy.54, f32[40,33,128]{2,1,0:T(8,128)S(1)} %copy-done.1, f32[40,33,128]{2,1,0:T(8,128)S(1)} %copy-done.2, f32[32,128]{1,0:T(8,128)S(1)} %get-tuple-element.157, ...), kind=kLoop, calls=%fused_computation.364 | loop fusion | flops 2621440 | bytes 4603904 | tf_op jit(solution)/shard_map/cond/branch_1_fun/add | solution.py:59
  71.9 0.4 fusion.169
  73.2 0.6 fusion.590
  73.8 0.7 copy.147
  74.5 0.9 collective-permute-start.15
  75.4 3.9 %collective-permute-done.15 = f32[1,32,128]{2,1,0:T(8,128)S(1)} collective-permute-done((f32[1,32,128]{2,1,0:T(8,128)}, f32[1,32,128]{2,1,0:T(8,128)S(1)}, u32[]{:S(2)}, u32[]{:S(2)}) %collective-permute-start.15) | collective-permute-done | bytes 16416 | tf_op jit(solution)/shard_map/ppermute | solution.py:25
  79.4 4.6 %collective-permute-done.16 = f32[1,32,128]{2,1,0:T(8,128)S(1)} collective-permute-done((f32[1,32,128]{2,1,0:T(8,128)S(1)}, f32[1,32,128]{2,1,0:T(8,128)S(1)}, u32[]{:S(2)}, u32[]{:S(2)}) %collective-permute-start.16) | collective-permute-done | bytes 16416 | tf_op jit(solution)/shard_map/ppermute | solution.py:25
  84.0 4.6 %collective-permute-done.17 = f32[1,32,128]{2,1,0:T(8,128)S(1)} collective-permute-done((f32[1,32,128]{2,1,0:T(8,128)S(1)}, f32[1,32,128]{2,1,0:T(8,128)S(1)}, u32[]{:S(2)}, u32[]{:S(2)}) %collective-permute-start.17) | collective-permute-done | bytes 16416 | tf_op jit(solution)/shard_map/ppermute | solution.py:25
  88.6 0.7 gather_fusion.1
  89.4 3.5 %collective-permute-start.18 = (f32[5,3,4,128]{3,2,1,0:T(4,128)S(1)}, f32[5,3,4,128]{3,2,1,0:T(4,128)S(1)}, u32[]{:S(2)}, u32[]{:S(2)}) collective-permute-start(f32[5,3,4,128]{3,2,1,0:T(4,128)S(1)} %get-tuple-element.462), channel_id=1, source_target_pairs={{0,2},{2,4},{4,6},{1,3},{3,5},{5,7},{8,10},{10,12},{12,14},{9,11},... | collective-permute-start | bytes 92168 | tf_op jit(solution)/shard_map/ppermute | solution.py:39
  92.9 1.3 %collective-permute-start.19 = (f32[5,3,4,128]{3,2,1,0:T(4,128)S(1)}, f32[5,3,4,128]{3,2,1,0:T(4,128)S(1)}, u32[]{:S(2)}, u32[]{:S(2)}) collective-permute-start(f32[5,3,4,128]{3,2,1,0:T(4,128)S(1)} %get-tuple-element.463), channel_id=1, source_target_pairs={{2,0},{4,2},{6,4},{3,1},{5,3},{7,5},{10,8},{12,10},{14,12},{11,9},... | collective-permute-start | bytes 92168 | tf_op jit(solution)/shard_map/ppermute | solution.py:41
  94.5 4.2 %collective-permute-done.19 = f32[5,3,4,128]{3,2,1,0:T(4,128)S(1)} collective-permute-done((f32[5,3,4,128]{3,2,1,0:T(4,128)S(1)}, f32[5,3,4,128]{3,2,1,0:T(4,128)S(1)}, u32[]{:S(2)}, u32[]{:S(2)}) %collective-permute-start.19) | collective-permute-done | bytes 30752 | tf_op jit(solution)/shard_map/ppermute | solution.py:41
  98.9 1.3 %collective-permute-start.20 = (f32[5,3,40,4]{3,2,1,0:T(8,128)S(1)}, f32[5,3,40,4]{3,2,1,0:T(8,128)S(1)}, u32[]{:S(2)}, u32[]{:S(2)}) collective-permute-start(f32[5,3,40,4]{3,2,1,0:T(8,128)S(1)} %get-tuple-element.458), channel_id=1, source_target_pairs={{0,1},{2,3},{4,5},{6,7},{8,9},{10,11},{12,13},{14,15},{16,17},{18,... | collective-permute-start | bytes 28808 | tf_op jit(solution)/shard_map/ppermute | solution.py:39
  100.2 1.3 %collective-permute-start.21 = (f32[5,3,40,4]{3,2,1,0:T(8,128)S(1)}, f32[5,3,40,4]{3,2,1,0:T(8,128)S(1)}, u32[]{:S(2)}, u32[]{:S(2)}) collective-permute-start(f32[5,3,40,4]{3,2,1,0:T(8,128)S(1)} %get-tuple-element.459), channel_id=1, source_target_pairs={{1,0},{3,2},{5,4},{7,6},{9,8},{11,10},{13,12},{15,14},{17,16},{19,... | collective-permute-start | bytes 28808 | tf_op jit(solution)/shard_map/ppermute | solution.py:41
  101.5 2.2 %collective-permute-done.21 = f32[5,3,40,4]{3,2,1,0:T(8,128)S(1)} collective-permute-done((f32[5,3,40,4]{3,2,1,0:T(8,128)S(1)}, f32[5,3,40,4]{3,2,1,0:T(8,128)S(1)}, u32[]{:S(2)}, u32[]{:S(2)}) %collective-permute-start.21) | collective-permute-done | bytes 9632 | tf_op jit(solution)/shard_map/ppermute | solution.py:41
  103.7 0.4 pad_maximum_fusion.6
  104.1 0.4 fusion.347
  104.5 0.4 fusion.334
  105.0 0.4 fusion.321
  105.6 1.3 %fusion.436 = f32[1,3,32,128]{3,2,1,0:T(8,128)} fusion(f32[3,32,128]{2,1,0:T(8,128)S(1)} %fusion.413, f32[1,32,128]{2,1,0:T(8,128)S(1)} %dynamic-slice_multiply_fusion, f32[1,32,128]{2,1,0:T(8,128)} %get-tuple-element.171, f32[1,32,128]{2,1,0:T(8,128)S(1)} %get-tuple-element.170, pred[]{:T(512)S(6)} %lt.32), kind=kLoop, calls=%fused_computation.944 | loop fusion | flops 36864 | bytes 147457 | tf_op jit(solution)/shard_map/broadcast_in_dim | solution.py:173
  (162 shorter events, 4.9 us)
Async XLA Ops:
  0.0 10.0 %collective-permute-start = (f32[40,1,128]{2,0,1:T(8,128)S(1)}, f32[40,1,128]{2,0,1:T(8,128)S(1)}, u32[]{:S(2)}, u32[]{:S(2)}) collective-permute-start(f32[40,1,128]{2,0,1:T(8,128)S(1)} %broadcast.6575), channel_id=1, source_target_pairs={{2,0},{4,2},{6,4},{3,1},{5,3},{7,5},{10,8},{12,10},{14,12},{11,9},... | collective-permute-start | bytes 61448 | tf_op jit(solution)/shard_map/ppermute | solution.py:41
  1.3 8.7 %collective-permute-start.1 = (f32[40,1,128]{2,0,1:T(8,128)S(1)}, f32[40,1,128]{2,0,1:T(8,128)S(1)}, u32[]{:S(2)}, u32[]{:S(2)}) collective-permute-start(f32[40,1,128]{2,0,1:T(8,128)S(1)} %broadcast.6575), channel_id=1, source_target_pairs={{0,2},{2,4},{4,6},{1,3},{3,5},{5,7},{8,10},{10,12},{12,14},{9,11},... | collective-permute-start | bytes 61448 | tf_op jit(solution)/shard_map/ppermute | solution.py:39
  10.6 4.7 %collective-permute-start.2 = (f32[40,34,1]{0,2,1:T(1,128)S(1)}, f32[40,34,1]{0,2,1:T(1,128)S(1)}, u32[]{:S(2)}, u32[]{:S(2)}) collective-permute-start(f32[40,34,1]{0,2,1:T(1,128)S(1)} %copy.56), channel_id=1, source_target_pairs={{1,0},{3,2},{5,4},{7,6},{9,8},{11,10},{13,12},{15,14},{17,16},{19,... | collective-permute-start | bytes 16328 | tf_op jit(solution)/shard_map/ppermute | solution.py:41
  12.2 3.9 %collective-permute-start.3 = (f32[40,34,1]{0,2,1:T(1,128)S(1)}, f32[40,34,1]{0,2,1:T(1,128)S(1)}, u32[]{:S(2)}, u32[]{:S(2)}) collective-permute-start(f32[40,34,1]{0,2,1:T(1,128)S(1)} %copy.57), channel_id=1, source_target_pairs={{0,1},{2,3},{4,5},{6,7},{8,9},{10,11},{12,13},{14,15},{16,17},{18,... | collective-permute-start | bytes 16328 | tf_op jit(solution)/shard_map/ppermute | solution.py:39
  21.2 21.5 %copy-start.5 = (f32[3,32,128]{2,1,0:T(8,128)S(1)}, f32[3,32,128]{2,1,0:T(8,128)}, u32[]{:S(2)}) copy-start(f32[3,32,128]{2,1,0:T(8,128)} %param.20) | copy-start | bytes 147460
  21.2 21.5 %copy-start.4 = (f32[3,32,128]{2,1,0:T(8,128)S(1)}, f32[3,32,128]{2,1,0:T(8,128)}, u32[]{:S(2)}) copy-start(f32[3,32,128]{2,1,0:T(8,128)} %param.21) | copy-start | bytes 147460
  21.2 21.5 %copy-start.6 = (f32[3,32,128]{2,1,0:T(8,128)S(1)}, f32[3,32,128]{2,1,0:T(8,128)}, u32[]{:S(2)}) copy-start(f32[3,32,128]{2,1,0:T(8,128)} %param.19) | copy-start | bytes 147460
  21.8 7.8 %collective-permute-start.8 = (f32[1,32,128]{2,1,0:T(8,128)S(1)}, f32[1,32,128]{2,1,0:T(8,128)S(1)}, u32[]{:S(2)}, u32[]{:S(2)}) collective-permute-start(f32[1,32,128]{2,1,0:T(8,128)S(1)} %get-tuple-element.447), channel_id=1, source_target_pairs={{0,8},{8,16},{16,24},{24,0},{1,9},{9,17},{17,25},{25,1},{2,10},{10... | collective-permute-start | bytes 49160 | tf_op jit(solution)/shard_map/ppermute | solution.py:25
  23.7 11.3 %collective-permute-start.4 = (f32[40,1,128]{0,2,1:T(8,128)S(1)}, f32[40,1,128]{0,2,1:T(8,128)S(1)}, u32[]{:S(2)}, u32[]{:S(2)}) collective-permute-start(f32[40,1,128]{0,2,1:T(8,128)S(1)} %get-tuple-element.439), channel_id=1, source_target_pairs={{2,0},{4,2},{6,4},{3,1},{5,3},{7,5},{10,8},{12,10},{14,12},{11,9},... | collective-permute-start | bytes 61448 | tf_op jit(solution)/shard_map/ppermute | solution.py:41
  25.0 10.0 %collective-permute-start.5 = (f32[40,1,128]{0,2,1:T(8,128)S(1)}, f32[40,1,128]{0,2,1:T(8,128)S(1)}, u32[]{:S(2)}, u32[]{:S(2)}) collective-permute-start(f32[40,1,128]{0,2,1:T(8,128)S(1)} %get-tuple-element.438), channel_id=1, source_target_pairs={{0,2},{2,4},{4,6},{1,3},{3,5},{5,7},{8,10},{10,12},{12,14},{9,11},... | collective-permute-start | bytes 61448 | tf_op jit(solution)/shard_map/ppermute | solution.py:39
  29.6 7.3 %copy-start.9 = (f32[1,32,128]{2,1,0:T(8,128)}, f32[1,32,128]{2,1,0:T(8,128)S(1)}, u32[]{:S(2)}) copy-start(f32[1,32,128]{2,1,0:T(8,128)S(1)} %collective-permute-done.8) | copy-start | bytes 49156
  29.6 4.8 %collective-permute-start.9 = (f32[1,32,128]{2,1,0:T(8,128)S(1)}, f32[1,32,128]{2,1,0:T(8,128)}, u32[]{:S(2)}, u32[]{:S(2)}) collective-permute-start(f32[1,32,128]{2,1,0:T(8,128)S(1)} %collective-permute-done.8), channel_id=1, source_target_pairs={{0,8},{8,16},{16,24},{24,0},{1,9},{9,17},{17,25},{25,1},{2,10},{10... | collective-permute-start | bytes 49160 | tf_op jit(solution)/shard_map/ppermute | solution.py:25
  31.2 11.6 %copy-start.10 = (s32[1024]{0:T(1024)}, s32[1024]{0:T(1024)S(1)}, u32[]{:S(2)}) copy-start(s32[1024]{0:T(1024)S(1)} %pad_clamp_fusion) | copy-start | bytes 12292
  34.4 6.9 %collective-permute-start.10 = (f32[1,32,128]{2,1,0:T(8,128)}, f32[1,32,128]{2,1,0:T(8,128)}, u32[]{:S(2)}, u32[]{:S(2)}) collective-permute-start(f32[1,32,128]{2,1,0:T(8,128)} %collective-permute-done.9), channel_id=1, source_target_pairs={{0,8},{8,16},{16,24},{24,0},{1,9},{9,17},{17,25},{25,1},{2,10},{10... | collective-permute-start | bytes 49160 | tf_op jit(solution)/shard_map/ppermute | solution.py:25
  35.0 6.3 %copy-start.8 = (f32[1,1,32,128]{3,2,1,0:T(8,128)S(1)}, f32[1,1,32,128]{3,2,1,0:T(8,128)}, u32[]{:S(2)}) copy-start(f32[1,1,32,128]{3,2,1,0:T(8,128)} %get-tuple-element.446) | copy-start | bytes 49156
  35.7 19.2 %collective-permute-start.6 = (f32[40,34,1]{0,2,1:T(1,128)}, f32[40,34,1]{0,2,1:T(1,128)}, u32[]{:S(2)}, u32[]{:S(2)}) collective-permute-start(f32[40,34,1]{0,2,1:T(1,128)} %get-tuple-element.437), channel_id=1, source_target_pairs={{1,0},{3,2},{5,4},{7,6},{9,8},{11,10},{13,12},{15,14},{17,16},{19,... | collective-permute-start | bytes 16328 | tf_op jit(solution)/shard_map/ppermute | solution.py:41
  37.0 17.9 %collective-permute-start.7 = (f32[40,34,1]{0,2,1:T(1,128)}, f32[40,34,1]{0,2,1:T(1,128)}, u32[]{:S(2)}, u32[]{:S(2)}) collective-permute-start(f32[40,34,1]{0,2,1:T(1,128)} %get-tuple-element.436), channel_id=1, source_target_pairs={{0,1},{2,3},{4,5},{6,7},{8,9},{10,11},{12,13},{14,15},{16,17},{18,... | collective-permute-start | bytes 16328 | tf_op jit(solution)/shard_map/ppermute | solution.py:39
  42.8 6.1 %collective-permute-start.11 = (f32[5,3,4,128]{3,2,1,0:T(4,128)S(1)}, f32[5,3,4,128]{3,2,1,0:T(4,128)S(1)}, u32[]{:S(2)}, u32[]{:S(2)}) collective-permute-start(f32[5,3,4,128]{3,2,1,0:T(4,128)S(1)} %get-tuple-element.464), channel_id=1, source_target_pairs={{0,2},{2,4},{4,6},{1,3},{3,5},{5,7},{8,10},{10,12},{12,14},{9,11},... | collective-permute-start | bytes 92168 | tf_op jit(solution)/shard_map/ppermute | solution.py:39
  46.3 5.8 %collective-permute-start.12 = (f32[5,3,4,128]{3,2,1,0:T(4,128)S(1)}, f32[5,3,4,128]{3,2,1,0:T(4,128)S(1)}, u32[]{:S(2)}, u32[]{:S(2)}) collective-permute-start(f32[5,3,4,128]{3,2,1,0:T(4,128)S(1)} %get-tuple-element.465), channel_id=1, source_target_pairs={{2,0},{4,2},{6,4},{3,1},{5,3},{7,5},{10,8},{12,10},{14,12},{11,9},... | collective-permute-start | bytes 92168 | tf_op jit(solution)/shard_map/ppermute | solution.py:41
  52.3 5.9 %collective-permute-start.13 = (f32[5,3,40,4]{3,2,1,0:T(8,128)S(1)}, f32[5,3,40,4]{3,2,1,0:T(8,128)S(1)}, u32[]{:S(2)}, u32[]{:S(2)}) collective-permute-start(f32[5,3,40,4]{3,2,1,0:T(8,128)S(1)} %get-tuple-element.460), channel_id=1, source_target_pairs={{0,1},{2,3},{4,5},{6,7},{8,9},{10,11},{12,13},{14,15},{16,17},{18,... | collective-permute-start | bytes 28808 | tf_op jit(solution)/shard_map/ppermute | solution.py:39
  53.6 4.6 %collective-permute-start.14 = (f32[5,3,40,4]{3,2,1,0:T(8,128)S(1)}, f32[5,3,40,4]{3,2,1,0:T(8,128)S(1)}, u32[]{:S(2)}, u32[]{:S(2)}) collective-permute-start(f32[5,3,40,4]{3,2,1,0:T(8,128)S(1)} %get-tuple-element.461), channel_id=1, source_target_pairs={{1,0},{3,2},{5,4},{7,6},{9,8},{11,10},{13,12},{15,14},{17,16},{19,... | collective-permute-start | bytes 28808 | tf_op jit(solution)/shard_map/ppermute | solution.py:41
  59.0 0.9 copy-start.3
  59.0 0.9 copy-start.7
  59.1 1.7 %copy-start = (f32[40,34,129]{0,2,1:T(8,128)S(1)}, f32[40,34,129]{0,2,1:T(8,128)}, u32[]{:S(2)}) copy-start(f32[40,34,129]{0,2,1:T(8,128)} %get-tuple-element.434) | copy-start | bytes 2105284
  67.4 1.1 %copy-start.1 = (f32[40,33,128]{2,1,0:T(8,128)S(1)}, f32[40,33,128]{2,1,0:T(8,128)}, u32[]{:S(2)}) copy-start(f32[40,33,128]{2,1,0:T(8,128)} %get-tuple-element.161) | copy-start | bytes 2027524 | tf_op jit(solution)/shard_map/cond
  67.4 1.4 %copy-start.2 = (f32[40,33,128]{2,1,0:T(8,128)S(1)}, f32[40,33,128]{2,1,0:T(8,128)}, u32[]{:S(2)}) copy-start(f32[40,33,128]{2,1,0:T(8,128)} %get-tuple-element.160) | copy-start | bytes 2027524 | tf_op jit(solution)/shard_map/cond
  74.5 4.8 %collective-permute-start.15 = (f32[1,32,128]{2,1,0:T(8,128)}, f32[1,32,128]{2,1,0:T(8,128)S(1)}, u32[]{:S(2)}, u32[]{:S(2)}) collective-permute-start(f32[1,32,128]{2,1,0:T(8,128)} %get-tuple-element.171), channel_id=1, source_target_pairs={{0,8},{8,16},{16,24},{24,0},{1,9},{9,17},{17,25},{25,1},{2,10},{10... | collective-permute-start | bytes 49160 | tf_op jit(solution)/shard_map/ppermute | solution.py:25
  79.3 4.6 %collective-permute-start.16 = (f32[1,32,128]{2,1,0:T(8,128)S(1)}, f32[1,32,128]{2,1,0:T(8,128)S(1)}, u32[]{:S(2)}, u32[]{:S(2)}) collective-permute-start(f32[1,32,128]{2,1,0:T(8,128)S(1)} %collective-permute-done.15), channel_id=1, source_target_pairs={{0,8},{8,16},{16,24},{24,0},{1,9},{9,17},{17,25},{25,1},{2,10},{10... | collective-permute-start | bytes 49160 | tf_op jit(solution)/shard_map/ppermute | solution.py:25
  84.0 4.6 %collective-permute-start.17 = (f32[1,32,128]{2,1,0:T(8,128)S(1)}, f32[1,32,128]{2,1,0:T(8,128)S(1)}, u32[]{:S(2)}, u32[]{:S(2)}) collective-permute-start(f32[1,32,128]{2,1,0:T(8,128)S(1)} %collective-permute-done.16), channel_id=1, source_target_pairs={{0,8},{8,16},{16,24},{24,0},{1,9},{9,17},{17,25},{25,1},{2,10},{10... | collective-permute-start | bytes 49160 | tf_op jit(solution)/shard_map/ppermute | solution.py:25
  89.4 5.0 %collective-permute-start.18 = (f32[5,3,4,128]{3,2,1,0:T(4,128)S(1)}, f32[5,3,4,128]{3,2,1,0:T(4,128)S(1)}, u32[]{:S(2)}, u32[]{:S(2)}) collective-permute-start(f32[5,3,4,128]{3,2,1,0:T(4,128)S(1)} %get-tuple-element.462), channel_id=1, source_target_pairs={{0,2},{2,4},{4,6},{1,3},{3,5},{5,7},{8,10},{10,12},{12,14},{9,11},... | collective-permute-start | bytes 92168 | tf_op jit(solution)/shard_map/ppermute | solution.py:39
  92.9 5.8 %collective-permute-start.19 = (f32[5,3,4,128]{3,2,1,0:T(4,128)S(1)}, f32[5,3,4,128]{3,2,1,0:T(4,128)S(1)}, u32[]{:S(2)}, u32[]{:S(2)}) collective-permute-start(f32[5,3,4,128]{3,2,1,0:T(4,128)S(1)} %get-tuple-element.463), channel_id=1, source_target_pairs={{2,0},{4,2},{6,4},{3,1},{5,3},{7,5},{10,8},{12,10},{14,12},{11,9},... | collective-permute-start | bytes 92168 | tf_op jit(solution)/shard_map/ppermute | solution.py:41
  98.9 2.6 %collective-permute-start.20 = (f32[5,3,40,4]{3,2,1,0:T(8,128)S(1)}, f32[5,3,40,4]{3,2,1,0:T(8,128)S(1)}, u32[]{:S(2)}, u32[]{:S(2)}) collective-permute-start(f32[5,3,40,4]{3,2,1,0:T(8,128)S(1)} %get-tuple-element.458), channel_id=1, source_target_pairs={{0,1},{2,3},{4,5},{6,7},{8,9},{10,11},{12,13},{14,15},{16,17},{18,... | collective-permute-start | bytes 28808 | tf_op jit(solution)/shard_map/ppermute | solution.py:39
  100.2 3.5 %collective-permute-start.21 = (f32[5,3,40,4]{3,2,1,0:T(8,128)S(1)}, f32[5,3,40,4]{3,2,1,0:T(8,128)S(1)}, u32[]{:S(2)}, u32[]{:S(2)}) collective-permute-start(f32[5,3,40,4]{3,2,1,0:T(8,128)S(1)} %get-tuple-element.459), channel_id=1, source_target_pairs={{1,0},{3,2},{5,4},{7,6},{9,8},{11,10},{13,12},{15,14},{17,16},{19,... | collective-permute-start | bytes 28808 | tf_op jit(solution)/shard_map/ppermute | solution.py:41
